TPU v7x, 512 devices: a whole 4x8x8 slice. The times are simulated.
512 devices in a mesh: dp: 128 (over y, z, core), feat: 4 (over x).
Axes of the slice: x: 4, y: 8, z: 8, core: 2. Of those that a mesh axis runs over, the one named last changes fastest.
Arguments:
- activations: bfloat16 [131072, 8192], P('dp', 'feat'), may hold values from -6 to 6
- cand_index: int32 [131072], P('dp'), may hold values from 0 to 127
- labels: int32 [8192], P('dp'), may hold values 0 or 1
- counts: int32 [128], P('dp'), may hold values from 1 to 64, as said below
Outputs:
- scores: float32 [131072, 128], P('dp', 'feat')
Inputs may be any that keep to these rules, and one draw needn't show every extreme that they name: `counts`: the fullest slab has all 64 prompt slots live.
All inputs are finite; a program needn't handle non-finite values. No bound on the sum of `labels` on one device may be relied on, other than what follows from the above.
Results may differ from a plain program's by a relative error of at most 0.0047.
Values may be sent and summed in bfloat16 or wider, within the bound.
A program may use at most 64 MiB of HBM per device.

v0:
```python
import jax
import jax.numpy as jnp
from jax import lax
from jax.sharding import PartitionSpec as P

CAND_DEV = 1
PER_PROMPT = 16
epsilon = 1e-06


def project(activations, dir_block):
    return lax.dot_general(
        activations, dir_block, (((1,), (1,)), ((), ())), preferred_element_type=jnp.float32
    )


def per_device(activations, cand_index, labels, counts):
    row_total = activations.shape[0]
    cand_total = CAND_DEV * lax.axis_size("dp")
    prompt_of = jnp.arange(row_total, dtype=jnp.int32) // PER_PROMPT
    live = prompt_of < counts[0]
    classes = jnp.repeat(labels, PER_PROMPT)
    cand_ids = jnp.arange(cand_total, dtype=jnp.int32)
    matches = (cand_index[None, :] == cand_ids[:, None]) & live[None, :]
    harmful_hits = matches & (classes[None, :] == 1)
    harmless_hits = matches & (classes[None, :] == 0)
    member = jnp.concatenate([harmful_hits, harmless_hits], axis=0).astype(jnp.bfloat16)
    class_sums = jnp.dot(member, activations, preferred_element_type=jnp.float32).reshape(
        2, cand_total, -1
    )
    class_counts = jnp.sum(member.astype(jnp.float32), axis=1).reshape(2, cand_total)
    owned_sums, owned_counts = (
        lax.psum_scatter(class_sums, "dp", scatter_dimension=1, tiled=True),
        lax.psum_scatter(class_counts, "dp", scatter_dimension=1, tiled=True),
    )
    harmful_mean = owned_sums[0] / jnp.maximum(owned_counts[0], 1.0)[:, None]
    harmless_mean = owned_sums[1] / jnp.maximum(owned_counts[1], 1.0)[:, None]
    raw_float = harmful_mean - harmless_mean
    raw_dir = raw_float.astype(jnp.bfloat16)
    squares = jnp.sum(jnp.square(raw_dir.astype(jnp.float32)), axis=1)
    total_sq = lax.psum(squares, "feat")
    inv_norm = lax.rsqrt(total_sq + epsilon).astype(jnp.bfloat16)
    dir_block = lax.all_gather(raw_dir, "dp", axis=0, tiled=True)
    inv_block = lax.all_gather(inv_norm, "dp", axis=0, tiled=True)
    partial_value = project(activations, dir_block) * inv_block.astype(jnp.float32)[None, :]
    return lax.psum_scatter(partial_value, "feat", scatter_dimension=1, tiled=True)


def solution(mesh):
    return jax.shard_map(
        per_device,
        mesh=mesh,
        in_specs=(P("dp", "feat"), P("dp"), P("dp"), P("dp")),
        out_specs=P("dp", "feat"),
        check_vma=False,
    )
```

profile of v0, /device:TPU:8, one launch (start us, length us, event | category | flops | bytes accessed | tf_op | source)
XLA Modules:
  0.0 619.2 jit_solution(13851311557933916579)
XLA Ops:
  6.5 0.0 all-reduce.5.cloned.1.call-start
  6.5 0.7 broadcast_compare_fusion.1
  7.2 0.1 broadcast_in_dim.4
  7.3 0.1 eq.43
  7.4 0.1 broadcast_in_dim.5
  7.4 0.1 eq.45
  8.2 0.9 fusion.5
  9.1 3.4 fusion.6
  12.5 0.0 copy-start
  12.5 2.9 copy.8
  15.5 0.0 all-reduce.5.cloned.1.call-update
  15.5 0.0 reduce-scatter.3.cloned.1.call-start
  15.5 0.0 copy-done
  15.5 0.6 fusion.12
  16.1 0.2 convert_reduce_fusion
  16.3 222.9 %all-reduce.2 = f32[2,128]{1,0:T(2,128)S(1)} all-reduce(f32[2,128]{1,0:T(2,128)S(1)} %bitcast.23), channel_id=4, replica_groups=mesh['dp'=128,'feat'=4] {'dp'}, use_global_device_ids=true, to_apply=%region_2.3.clone | all-reduce | flops 256 | bytes 2048
  239.2 0.7 constant_dynamic-slice_fusion
  239.9 0.6 fusion.13
  241.8 0.0 all-reduce.5.cloned.1.call-done
  241.8 2.0 multiply_reduce_fusion
  243.9 11.3 %psum.7 = f32[1]{0:T(128)} all-reduce(f32[1]{0:T(128)} %bitcast.6), channel_id=1, replica_groups=mesh['dp'=128,'feat'=4] {'feat'}, use_global_device_ids=true, to_apply=%region_4.5 | all-reduce | flops 1 | bytes 8 | tf_op jit(solution)/shard_map/psum | solution.py:41
  256.4 1.3 dynamic-update-slice
  257.7 247.1 %all-reduce = bf16[128]{0:T(256)(128)(2,1)S(1)} all-reduce(bf16[128]{0:T(256)(128)(2,1)S(1)} %dynamic-update-slice), channel_id=1, replica_groups=mesh['dp'=128,'feat'=4] {'dp'}, use_global_device_ids=true, to_apply=%add | all-reduce | flops 128 | bytes 512
  504.8 83.2 %all-gather = bf16[128,1,2048]{2,1,0:T(2,128)(2,1)S(1)} all-gather(bf16[1,1,2048]{2,1,0:T(2,128)(2,1)S(1)} %bitcast.22), channel_id=2, replica_groups=mesh['dp'=128,'feat'=4] {'dp'}, dimensions={0}, use_global_device_ids=true | all-gather | bytes 528384 | tf_op jit(solution)/shard_map/all_gather | solution.py:43
  588.0 4.6 fusion
  592.5 0.0 reduce-scatter.3.cloned.1.call-update
  592.5 19.8 %reduce-scatter.3.cloned.1.call-done = f32[1024,32]{0,1:T(8,128)} async-done(((f32[1024,128]{0,1:T(8,128)}), f32[1024,32]{0,1:T(8,128)}) %reduce-scatter.3.cloned.1.call-update) | async-done | bytes 131088 | tf_op jit(solution)/shard_map/reduce_scatter | solution.py:46
  (3 shorter events, 0.0 us)
Async XLA Ops:
  6.5 235.3 %all-reduce.5.cloned.1.call-start = ((), (), s32[]{:S(2)}) async-start(), calls=%async_computation.2 | async-start | bytes 4194304
  12.5 3.0 copy-start
  15.5 596.9 %reduce-scatter.3.cloned.1.call-start = ((), (), s32[]{:S(2)}) async-start(), calls=%async_computation.1 | async-start | bytes 655360 | tf_op jit(solution)/shard_map/reduce_scatter | solution.py:46
Sparse Core Ops, SparseCore 0:
  15.6 204.9 all-reduce.4
  592.7 19.6 reduce-scatter.2
where the time goes:
time: 620 us; the launch traced here: 619 us
  blocking collectives  564 us (91%)
  waiting for transfers between devices  19.9 us (3%)
  between operations  16.6 us (3%)
  matrix products  8.01 us (1%)
  local copies, waits for them, and re-layouts  6.46 us (1%)
    unnamed x2, blocking collectives  470 us
    all_gather x1, blocking collectives, per_device(): dir_block = lax.all_gather(raw_dir, 'dp', axis=0, tiled=True)  83.2 us
    reduce_scatter x1, waiting for transfers between devices, per_device(): lax.psum_scatter(partial_value, 'feat', scatter_dimension=1, tiled=True)  19.8 us
  transfers between devices with their start and end apart: 2, of which 1 were waited for; matrix products, arithmetic and copies ran while one was open for 0% of the time, Pallas kernels for 0%

commit v1 on v0

--- a/solution.py
+++ b/solution.py
@@ -40,7 +40,9 @@
     squares = jnp.sum(jnp.square(raw_dir.astype(jnp.float32)), axis=1)
     total_sq = lax.psum(squares, "feat")
     inv_norm = lax.rsqrt(total_sq + epsilon).astype(jnp.bfloat16)
-    dir_block = lax.all_gather(raw_dir, "dp", axis=0, tiled=True)
+    dir_block = jnp.concatenate(
+        lax.all_to_all(jnp.stack([raw_dir] * lax.axis_size("dp")), "dp", 0, 0), axis=0
+    )
     inv_block = lax.all_gather(inv_norm, "dp", axis=0, tiled=True)
     partial_value = project(activations, dir_block) * inv_block.astype(jnp.float32)[None, :]
     return lax.psum_scatter(partial_value, "feat", scatter_dimension=1, tiled=True)

time: 620 us -> 586 us (0.945)
  blocking collectives: 564 us -> 450 us
  starting transfers between devices: 0.04 us -> 41.4 us
  waiting for transfers between devices: 19.9 us -> 53.3 us
    all_gather x1 -> x0, blocking collectives: 83.2 us -> none  [per_device(): dir_block = lax.all_gather(raw_dir, 'dp', axis=0, tiled=True)]
    all_to_all x0 -> x1, starting transfers between devices: none -> 41.3 us  [per_device(): lax.all_to_all(jnp.stack([raw_dir] * lax.axis_size('dp')), 'dp', 0, 0)]
    reduce_scatter x1, waiting for transfers between devices: 19.8 us -> 53.3 us  [per_device(): lax.psum_scatter(partial_value, 'feat', scatter_dimension=1, tiled=True)]
    unnamed x2, blocking collectives: 470 us -> 438 us
  transfers between devices with their start and end apart: 2 -> 3, of which waited for: 1 -> 1; matrix products, arithmetic and copies ran while one was open for 0% -> 1% of each run, Pallas kernels for 0% -> 0%
where the time goes in v1:
time: 586 us
  blocking collectives  450 us (77%)
  waiting for transfers between devices  53.3 us (9%)
  starting transfers between devices  41.4 us (7%)
  between operations  16.6 us (3%)
  local copies, waits for them, and re-layouts  9.26 us (2%)
  matrix products  7.97 us (1%)
  other arithmetic  7.5 us (1%)
    unnamed x2, blocking collectives  438 us
    reduce_scatter x1, waiting for transfers between devices, per_device(): lax.psum_scatter(partial_value, 'feat', scatter_dimension=1, tiled=True)  53.3 us
    all_to_all x1, starting transfers between devices, per_device(): lax.all_to_all(jnp.stack([raw_dir] * lax.axis_size('dp')), 'dp', 0, 0)  41.3 us
  transfers between devices with their start and end apart: 3, of which 1 were waited for; matrix products, arithmetic and copies ran while one was open for 1% of the time, Pallas kernels for 0%

profile of v1, /device:TPU:8, one launch (start us, length us, event | category | flops | bytes accessed | tf_op | source)
XLA Modules:
  0.0 585.6 jit_solution(10711074382660551600)
XLA Ops:
  6.5 0.7 broadcast_compare_fusion.1
  7.2 0.1 broadcast_in_dim.4
  7.3 0.1 eq.43
  7.4 0.1 broadcast_in_dim.5
  7.4 0.1 eq.45
  8.2 0.9 fusion.5
  9.1 3.4 fusion.6
  12.5 0.0 copy-start
  12.5 2.9 copy.6
  15.5 0.0 all-reduce.5.cloned.1.call-update
  15.5 0.0 copy-done
  15.5 0.6 fusion.12
  16.1 0.2 convert_reduce_fusion
  16.3 222.8 %all-reduce.2 = f32[2,128]{1,0:T(2,128)S(1)} all-reduce(f32[2,128]{1,0:T(2,128)S(1)} %bitcast.19), channel_id=3, replica_groups=mesh['dp'=128,'feat'=4] {'dp'}, use_global_device_ids=true, to_apply=%region_2.3.clone | all-reduce | flops 256 | bytes 2048
  239.1 0.7 constant_dynamic-slice_fusion
  239.7 0.6 fusion.13
  241.6 0.0 all-reduce.5.cloned.1.call-done
  241.6 2.0 multiply_reduce_fusion
  243.7 0.5 stack.5
  244.3 0.6 broadcast.88
  244.9 3.7 reduce.4
  248.6 1.2 reshape.124
  249.8 41.3 %all-to-all-start = ((bf16[128,2,1024]{2,1,0:T(2,128)(2,1)}), bf16[128,2,1024]{2,1,0:T(2,128)(2,1)S(1)}, u32[]{:S(2)}, u32[]{:S(2)}) async-start(bf16[128,2,1024]{2,1,0:T(2,128)(2,1)} %reshape.124), calls=%async_computation | async-start | bytes 1048576 | tf_op jit(solution)/shard_map/all_to_all | solution.py:44
  291.1 0.0 reduce-scatter.3.cloned.1.call-start
  291.2 11.2 %psum.7 = f32[1]{0:T(128)} all-reduce(f32[1]{0:T(128)} %bitcast.5), channel_id=1, replica_groups=mesh['dp'=128,'feat'=4] {'feat'}, use_global_device_ids=true, to_apply=%region_4.5 | all-reduce | flops 1 | bytes 8 | tf_op jit(solution)/shard_map/psum | solution.py:41
  303.6 1.3 dynamic-update-slice
  304.9 215.6 %all-reduce = bf16[128]{0:T(256)(128)(2,1)S(1)} all-reduce(bf16[128]{0:T(256)(128)(2,1)S(1)} %dynamic-update-slice), channel_id=1, replica_groups=mesh['dp'=128,'feat'=4] {'dp'}, use_global_device_ids=true, to_apply=%add | all-reduce | flops 128 | bytes 512
  520.4 0.0 all-to-all-done
  520.5 0.5 reshape.125
  520.9 4.5 fusion
  525.4 0.0 reduce-scatter.3.cloned.1.call-update
  525.5 53.3 %reduce-scatter.3.cloned.1.call-done = f32[1024,32]{0,1:T(8,128)} async-done(((f32[1024,128]{0,1:T(8,128)}), f32[1024,32]{0,1:T(8,128)}) %reduce-scatter.3.cloned.1.call-update) | async-done | bytes 131088 | tf_op jit(solution)/shard_map/reduce_scatter | solution.py:48
  (5 shorter events, 0.1 us)
Async XLA Ops:
  6.5 235.1 %all-reduce.5.cloned.1.call-start = ((), (), s32[]{:S(2)}) async-start(), calls=%async_computation.3 | async-start | bytes 4194304
  12.5 3.0 copy-start
  249.8 270.7 %all-to-all-start = ((bf16[128,2,1024]{2,1,0:T(2,128)(2,1)}), bf16[128,2,1024]{2,1,0:T(2,128)(2,1)S(1)}, u32[]{:S(2)}, u32[]{:S(2)}) async-start(bf16[128,2,1024]{2,1,0:T(2,128)(2,1)} %reshape.124), calls=%async_computation | async-start | bytes 1048576 | tf_op jit(solution)/shard_map/all_to_all | solution.py:44
  291.1 287.6 %reduce-scatter.3.cloned.1.call-start = ((), (), s32[]{:S(2)}) async-start(), calls=%async_computation.2 | async-start | bytes 655360 | tf_op jit(solution)/shard_map/reduce_scatter | solution.py:48
Sparse Core Ops, SparseCore 0:
  15.6 204.6 all-reduce.4
  525.6 53.1 reduce-scatter.2
